TPU v7x, 32 devices: a whole 2x2x4 slice. The times are simulated.
32 devices in a mesh: gx: 4 (over y, core), gy: 8 (over z, x).
Axes of the slice: x: 2, y: 2, z: 4, core: 2. Of those that a mesh axis runs over, the one named last changes fastest.
Arguments:
- tokens: bfloat16 [4, 256, 6144], P('gx', None, 'gy'), may hold values from -6 to 6
- norm_gain: float32 [6144], replicated, may hold values from 0.1 to 1.9
- qkv_weight: bfloat16 [6144, 3, 4096], P('gx', None, 'gy'), may hold values from -0.078125 to 0.078125
- up_weight: bfloat16 [6144, 24576], P('gx', 'gy'), may hold values from -0.078125 to 0.078125
- query_gain: float32 [128], replicated, may hold values from 0.1 to 1.9
- key_gain: float32 [128], replicated, may hold values from 0.1 to 1.9
- out_weight: bfloat16 [4096, 6144], P('gy', 'gx'), may hold values from -0.09375 to 0.09375
- down_weight: bfloat16 [24576, 6144], P('gy', 'gx'), may hold values from -0.0390625 to 0.0390625
- attention_keep: int32 [4, 256, 6144], P('gx', None, 'gy'), may hold values 0 or 1
- feedforward_keep: int32 [4, 256, 6144], P('gx', None, 'gy'), may hold values 0 or 1
Outputs:
- block_out: bfloat16 [4, 256, 6144], P('gx', None, 'gy')
All inputs are finite; a program needn't handle non-finite values. No bound on the sum of `attention_keep` or of `feedforward_keep` on one device may be relied on, other than what follows from the above.
Results may differ from a plain program's by a relative error of at most 0.017.
Values may be sent and summed in bfloat16 or wider, within the bound.
A program may use at most 128 MiB of HBM per device.

v0:
```python
import jax
import jax.numpy as jnp
from jax import lax
from jax.sharding import PartitionSpec as P

epsilon = 1e-06
keep_scale = 1.0 / 0.9


def layer_norm(values, gain):
    center = values - jnp.mean(values, axis=-1, keepdims=True)
    variance = jnp.mean(center * center, axis=-1, keepdims=True)
    return center * lax.rsqrt(variance + epsilon) * gain


def head_norm(values, gain):
    row_count = values.shape[0]
    shaped = values.reshape(row_count, -1, gain.shape[0])
    return layer_norm(shaped, gain).reshape(row_count, -1)


def per_device(
    tokens,
    norm_gain,
    qkv_weight,
    up_weight,
    query_gain,
    key_gain,
    out_weight,
    down_weight,
    attention_keep,
    feedforward_keep,
):
    images, seq_len, slice_width = tokens.shape
    whole_rows = lax.all_gather(tokens, "gy", axis=2, tiled=True)
    model_width = whole_rows.shape[2]
    own_rows = images * seq_len
    normed = (
        layer_norm(whole_rows.astype(jnp.float32), norm_gain)
        .astype(jnp.bfloat16)
        .reshape(own_rows, model_width)
    )
    blocks = lax.all_to_all(normed, "gx", split_axis=1, concat_axis=0, tiled=True)
    block_width = blocks.shape[1]
    head_cols = qkv_weight.shape[2]
    head_size = query_gain.shape[0]
    qkv_flat = qkv_weight.reshape(block_width, 3 * head_cols)
    joined = jnp.concatenate([qkv_flat, up_weight], axis=1)
    united = lax.psum_scatter(
        jnp.dot(blocks, joined, preferred_element_type=jnp.float32).astype(jnp.bfloat16),
        "gx",
        scatter_dimension=0,
        tiled=True,
    ).astype(jnp.float32)
    queries = head_norm(united[:, :head_cols], query_gain).astype(jnp.bfloat16)
    keys = head_norm(united[:, head_cols : 2 * head_cols], key_gain).astype(jnp.bfloat16)
    values = united[:, 2 * head_cols : 3 * head_cols].astype(jnp.bfloat16)
    hidden = jax.nn.gelu(united[:, 3 * head_cols :], approximate=False).astype(jnp.bfloat16)
    query_grid = queries.reshape(images, seq_len, -1, head_size)
    key_grid = keys.reshape(images, seq_len, -1, head_size)
    value_grid = values.reshape(images, seq_len, -1, head_size)
    scores = jnp.einsum(
        "bshd,bthd->bhst", query_grid, key_grid, preferred_element_type=jnp.float32
    ) * head_size ** (-0.5)
    raised = jnp.exp(scores)
    weights = (raised / jnp.sum(raised, axis=-1, keepdims=True)).astype(jnp.bfloat16)
    attended = jnp.einsum(
        "bhst,bthd->bshd", weights, value_grid, preferred_element_type=jnp.float32
    )
    attended = attended.astype(jnp.bfloat16).reshape(own_rows, head_cols)
    attention_part = jnp.dot(
        lax.all_gather(attended, "gx", axis=0, tiled=True),
        out_weight,
        preferred_element_type=jnp.float32,
    )
    feedforward_part = jnp.dot(
        lax.all_gather(hidden, "gx", axis=0, tiled=True),
        down_weight,
        preferred_element_type=jnp.float32,
    )
    delivered = (
        lax.all_to_all(
            attention_part.astype(jnp.bfloat16), "gx", split_axis=0, concat_axis=1, tiled=True
        ),
        lax.all_to_all(
            feedforward_part.astype(jnp.bfloat16), "gx", split_axis=0, concat_axis=1, tiled=True
        ),
    )
    rounded = jnp.stack([delivered[0], delivered[1]])
    rounded = lax.optimization_barrier(rounded)
    totals = lax.psum_scatter(
        rounded.astype(jnp.float32).astype(jnp.bfloat16), "gy", scatter_dimension=2, tiled=True
    ).astype(jnp.float32)
    attention_out = totals[0].reshape(images, seq_len, slice_width)
    feedforward_out = totals[1].reshape(images, seq_len, slice_width)
    branches = (
        attention_keep.astype(jnp.float32) * attention_out
        + feedforward_keep.astype(jnp.float32) * feedforward_out
    )
    return (tokens.astype(jnp.float32) + branches * keep_scale).astype(jnp.bfloat16)


def solution(mesh):
    in_specs = (
        P("gx", None, "gy"),
        P(),
        P("gx", None, "gy"),
        P("gx", "gy"),
        P(),
        P(),
        P("gy", "gx"),
        P("gy", "gx"),
        P("gx", None, "gy"),
        P("gx", None, "gy"),
    )
    out_specs = P("gx", None, "gy")
    return jax.shard_map(
        per_device, mesh=mesh, in_specs=in_specs, out_specs=out_specs, check_vma=False
    )
```

profile of v0, /device:TPU:0, one launch (start us, length us, event | category | flops | bytes accessed | tf_op | source)
XLA Modules:
  0.0 534.5 jit_solution(1531559722905003716)
XLA Ops:
  6.5 2.0 copy.26
  8.6 63.7 %all-gather.4.cloned.1.call-done = bf16[1,256,6144]{1,2,0:T(8,128)(2,1)} async-done(((bf16[1,256,768]{1,2,0:T(8,128)(2,1)}), bf16[1,256,6144]{1,2,0:T(8,128)(2,1)}) %all-gather.4.cloned.1.call-update) | async-done | bytes 3145744 | tf_op jit(solution)/shard_map/all_gather | solution.py:35
  72.3 2.9 convert_reduce_fusion
  75.2 0.9 fusion.9
  76.1 2.3 fusion.11
  78.3 4.7 all-to-all-start
  83.1 6.6 %copy.28 = bf16[1536,3,512]{0,2,1:T(8,128)(2,1)} copy(bf16[1536,3,512]{2,0,1:T(8,128)(2,1)} %param.12) | data formatting | bytes 9437184 | tf_op args[2]
  89.7 6.6 %copy.29 = bf16[1536,1536]{1,0:T(8,128)(2,1)} copy(bf16[1536,1536]{0,1:T(8,128)(2,1)} %bitcast.67) | data formatting | bytes 9437184 | tf_op jit(solution)/shard_map/reshape | solution.py:47
  96.3 23.7 %all-to-all-done = bf16[256,4,1536]{0,2,1:T(8,128)(2,1)} async-done(((bf16[256,4,1536]{0,2,1:T(8,128)(2,1)}), bf16[256,4,1536]{0,2,1:T(8,128)(2,1)}, u32[]{:S(2)}, u32[]{:S(2)}) %all-to-all-start) | async-done | bytes 3145760 | tf_op jit(solution)/shard_map/all_to_all | solution.py:43
  120.0 4.7 copy.27
  124.6 22.6 %fusion.4 = bf16[1024,4608]{1,0:T(8,128)(2,1)} fusion(bf16[1024,1536]{1,0:T(8,128)(2,1)} %bitcast.71, bf16[1536,3072]{1,0:T(8,128)(2,1)} %param.13, bf16[1536,1536]{1,0:T(8,128)(2,1)} %copy.29), kind=kOutput, calls=%fused_computation.4 | convolution fusion | flops 14528544768 | bytes 26738688 | tf_op jit(solution)/shard_map/dot_general | solution.py:50
  148.0 75.2 %reduce-scatter.3.cloned.1.call-done = bf16[256,4608]{1,0:T(8,128)(2,1)} async-done(((bf16[1024,4608]{1,0:T(8,128)(2,1)}), bf16[256,4608]{1,0:T(8,128)(2,1)}) %reduce-scatter.3.cloned.1.call-update) | async-done | bytes 2359312 | tf_op jit(solution)/shard_map/reduce_scatter | solution.py:49
  223.2 1.2 fusion.40
  224.9 0.6 multiply_reduce_fusion
  227.0 2.2 convert_element_type.63
  231.6 1.0 convolution_convert_fusion.2
  232.7 8.6 %fusion.14 = bf16[256,3072]{1,0:T(8,128)(2,1)} fusion(f32[256,4608]{1,0:T(8,128)} %copy-done.3), kind=kLoop, calls=%fused_computation.18 | loop fusion | flops 51118080 | bytes 4718592 | tf_op jit(solution)/shard_map/convert_element_type | solution.py:58
  241.3 8.3 %all-gather.6.cloned.1.call-done = bf16[1024,512]{0,1:T(8,128)(2,1)} async-done(((bf16[256,512]{0,1:T(8,128)(2,1)}), bf16[1024,512]{0,1:T(8,128)(2,1)}) %all-gather.6.cloned.1.call-update) | async-done | bytes 1048592 | tf_op jit(solution)/shard_map/all_gather | solution.py:72
  249.6 4.7 convolution_convert_fusion.1
  254.3 4.7 all-to-all-start.1
  259.1 72.0 %all-gather.8.cloned.1.call-done = bf16[1024,3072]{1,0:T(8,128)(2,1)} async-done(((bf16[256,3072]{1,0:T(8,128)(2,1)}), bf16[1024,3072]{1,0:T(8,128)(2,1)}) %all-gather.8.cloned.1.call-update) | async-done | bytes 6291472 | tf_op jit(solution)/shard_map/all_gather | solution.py:77
  331.1 15.6 %convolution_convert_fusion = bf16[1024,1536]{1,0:T(8,128)(2,1)} fusion(bf16[1024,3072]{1,0:T(8,128)(2,1)} %all-gather.8.cloned.1.call-done, bf16[3072,1536]{1,0:T(8,128)(2,1)} %param.17), kind=kOutput, calls=%fused_computation.14 | convolution fusion | flops 9665249280 | bytes 18874368 | tf_op jit(solution)/shard_map/dot_general | solution.py:76
  346.6 4.9 all-to-all-start.2
  351.6 6.0 %copy.34 = bf16[256,4,1536]{2,1,0:T(4,128)(2,1)} copy(bf16[256,4,1536]{2,0,1:T(8,128)(2,1)} %bitcast.11) | data formatting | bytes 6291456 | tf_op jit(solution)/shard_map/all_to_all | solution.py:82
  357.6 6.9 %stack.9 = bf16[1,256,6144]{2,1,0:T(8,128)(2,1)} reshape(bf16[256,4,1536]{2,1,0:T(4,128)(2,1)} %copy.34) | data formatting | bytes 6291456 | tf_op jit(solution)/shard_map/stack | solution.py:89
  364.5 24.0 %all-to-all-done.2 = bf16[4,256,1536]{2,1,0:T(8,128)(2,1)} async-done(((bf16[4,256,1536]{2,1,0:T(8,128)(2,1)}), bf16[4,256,1536]{2,1,0:T(8,128)(2,1)}, u32[]{:S(2)}, u32[]{:S(2)}) %all-to-all-start.2) | async-done | bytes 3145760 | tf_op jit(solution)/shard_map/all_to_all | solution.py:85
  388.5 6.0 %copy.35 = bf16[256,4,1536]{2,1,0:T(4,128)(2,1)} copy(bf16[256,4,1536]{2,0,1:T(8,128)(2,1)} %bitcast.13) | data formatting | bytes 6291456 | tf_op jit(solution)/shard_map/all_to_all | solution.py:85
  394.5 6.9 %stack.10 = bf16[1,256,6144]{2,1,0:T(8,128)(2,1)} reshape(bf16[256,4,1536]{2,1,0:T(4,128)(2,1)} %copy.35) | data formatting | bytes 6291456 | tf_op jit(solution)/shard_map/stack | solution.py:89
  401.4 6.1 %pad_maximum_fusion = bf16[2,256,6144]{2,1,0:T(8,128)(2,1)} fusion(bf16[1,256,6144]{2,1,0:T(8,128)(2,1)} %stack.10, bf16[1,256,6144]{2,1,0:T(8,128)(2,1)} %stack.9), kind=kLoop, calls=%fused_computation.12 | loop fusion | flops 3145728 | bytes 12582912 | tf_op jit(solution)/shard_map/stack | solution.py:89
  407.5 118.2 %reduce-scatter.5.cloned.1.call-done = bf16[2,256,768]{2,1,0:T(8,128)(2,1)} async-done(((bf16[2,256,6144]{2,1,0:T(8,128)(2,1)}), bf16[2,256,768]{2,1,0:T(8,128)(2,1)}) %reduce-scatter.5.cloned.1.call-update) | async-done | bytes 786448 | tf_op jit(solution)/shard_map/reduce_scatter | solution.py:91
  525.7 1.2 convert_element_type.73
  527.0 1.0 fusion.26
  (52 shorter events, 5.2 us)
Async XLA Ops:
  6.5 243.1 %copy-start = (bf16[512,1536]{1,0:T(8,128)(2,1)S(1)}, bf16[512,1536]{1,0:T(8,128)(2,1)}, u32[]{:S(2)}) copy-start(bf16[512,1536]{1,0:T(8,128)(2,1)} %param.16) | copy-start | bytes 4718596
  6.5 65.7 %all-gather.4.cloned.1.call-start = ((), (), s32[]{:S(2)}) async-start(), calls=%async_computation.5 | async-start | bytes 3538944 | tf_op jit(solution)/shard_map/all_gather | solution.py:35
  72.3 2.9 copy-start.2
  72.3 3.8 copy-start.7
  78.3 41.7 %all-to-all-start = ((bf16[256,4,1536]{0,2,1:T(8,128)(2,1)}), bf16[256,4,1536]{0,2,1:T(8,128)(2,1)}, u32[]{:S(2)}, u32[]{:S(2)}) async-start(bf16[256,4,1536]{0,2,1:T(8,128)(2,1)} %bitcast.68), calls=%async_computation | async-start | bytes 6291456 | tf_op jit(solution)/shard_map/all_to_all | solution.py:43
  83.0 140.2 %reduce-scatter.3.cloned.1.call-start = ((), (), s32[]{:S(2)}) async-start(), calls=%async_computation.6 | async-start | bytes 11796480 | tf_op jit(solution)/shard_map/reduce_scatter | solution.py:49
  147.3 0.7 copy-start.8
  147.3 0.7 copy-start.9
  147.3 102.3 %all-gather.6.cloned.1.call-start = ((), (), s32[]{:S(2)}) async-start(), calls=%async_computation.7 | async-start | bytes 1310720 | tf_op jit(solution)/shard_map/all_gather | solution.py:72
  224.3 2.5 slice-start
  229.2 2.1 copy-start.3
  232.7 98.4 %all-gather.8.cloned.1.call-start = ((), (), s32[]{:S(2)}) async-start(), calls=%async_computation.8 | async-start | bytes 7864320 | tf_op jit(solution)/shard_map/all_gather | solution.py:77
  254.3 92.3 %all-to-all-start.1 = ((bf16[4,256,1536]{2,1,0:T(8,128)(2,1)}), bf16[4,256,1536]{2,1,0:T(8,128)(2,1)}, u32[]{:S(2)}, u32[]{:S(2)}) async-start(bf16[4,256,1536]{2,1,0:T(8,128)(2,1)} %bitcast.70), calls=%async_computation.2 | async-start | bytes 6291456 | tf_op jit(solution)/shard_map/all_to_all | solution.py:82
  346.6 41.8 %all-to-all-start.2 = ((bf16[4,256,1536]{2,1,0:T(8,128)(2,1)}), bf16[4,256,1536]{2,1,0:T(8,128)(2,1)}, u32[]{:S(2)}, u32[]{:S(2)}) async-start(bf16[4,256,1536]{2,1,0:T(8,128)(2,1)} %bitcast.69), calls=%async_computation.3 | async-start | bytes 6291456 | tf_op jit(solution)/shard_map/all_to_all | solution.py:85
  351.5 174.2 %reduce-scatter.5.cloned.1.call-start = ((), (), s32[]{:S(2)}) async-start(), calls=%async_computation.9 | async-start | bytes 7077888 | tf_op jit(solution)/shard_map/reduce_scatter | solution.py:91
  407.5 119.4 %copy-start.4 = (bf16[1,256,768]{2,1,0:T(8,128)(2,1)S(1)}, bf16[1,256,768]{2,1,0:T(8,128)(2,1)}, u32[]{:S(2)}) copy-start(bf16[1,256,768]{2,1,0:T(8,128)(2,1)} %param.10) | copy-start | bytes 1179652
  407.5 119.5 %copy-start.5 = (s32[1,256,768]{2,1,0:T(8,128)S(1)}, s32[1,256,768]{2,1,0:T(8,128)}, u32[]{:S(2)}) copy-start(s32[1,256,768]{2,1,0:T(8,128)} %param.19) | copy-start | bytes 2359300
  407.5 119.5 %copy-start.6 = (s32[1,256,768]{2,1,0:T(8,128)S(1)}, s32[1,256,768]{2,1,0:T(8,128)}, u32[]{:S(2)}) copy-start(s32[1,256,768]{2,1,0:T(8,128)} %param.18) | copy-start | bytes 2359300
  407.5 120.4 %copy-start.1 = (bf16[512,1536]{1,0:T(8,128)(2,1)S(1)}, bf16[512,1536]{1,0:T(8,128)(2,1)}, u32[]{:S(2)}) copy-start(bf16[512,1536]{1,0:T(8,128)(2,1)} %param.16) | copy-start | bytes 4718596
Sparse Core Ops, SparseCore 0:
  9.5 62.7 all-gather.3
  147.4 75.6 reduce-scatter.2
  232.8 16.8 all-gather.5
  251.0 79.9 all-gather.7
  407.6 118.0 reduce-scatter.4
where the time goes:
time: 536 us; the launch traced here: 534 us
  waiting for transfers between devices  385 us (72%)
  local copies, waits for them, and re-layouts  49.6 us (9%)
  matrix products  44.2 us (8%)
  other arithmetic  27.6 us (5%)
  starting transfers between devices  14.6 us (3%)
  between operations  13.4 us (2%)
    reduce_scatter x1, waiting for transfers between devices, per_device(): lax.psum_scatter(rounded.astype(jnp.float32).astype(jnp.bfloat16), 'gy',...  118 us
    reduce_scatter x1, waiting for transfers between devices, per_device(): lax.psum_scatter(jnp.dot(blocks, joined, preferred_element_type=jnp.float...  75.2 us
    all_gather x1, waiting for transfers between devices, per_device(): lax.all_gather(hidden, 'gx', axis=0, tiled=True)  72 us
    all_gather x1, waiting for transfers between devices, per_device(): whole_rows = lax.all_gather(tokens, 'gy', axis=2, tiled=True)  63.7 us
    all_to_all x1, waiting for transfers between devices, per_device(): lax.all_to_all(feedforward_part.astype(jnp.bfloat16), 'gx', split_axis=0,...  24 us
    all_to_all x1, waiting for transfers between devices, per_device(): lax.all_to_all(normed, 'gx', split_axis=1, concat_axis=0, tiled=True)  23.7 us
    dot_general x1, matrix products, per_device(): jnp.dot(blocks, joined, preferred_element_type=jnp.float32)  22.6 us
    dot_general x1, matrix products, per_device(): jnp.dot(lax.all_gather(hidden, 'gx', axis=0, tiled=True), down_weight, pr...  15.6 us
  transfers between devices with their start and end apart: 8, of which 7 were waited for; matrix products, arithmetic and copies ran while one was open for 10% of the time, Pallas kernels for 0%

commit v1 on v0

--- a/solution.py
+++ b/solution.py
@@ -32,7 +32,9 @@
     feedforward_keep,
 ):
     images, seq_len, slice_width = tokens.shape
-    whole_rows = lax.all_gather(tokens, "gy", axis=2, tiled=True)
+    whole_rows = jnp.concatenate(
+        lax.all_to_all(jnp.stack([tokens] * lax.axis_size("gy")), "gy", 0, 0), axis=2
+    )
     model_width = whole_rows.shape[2]
     own_rows = images * seq_len
     normed = (

time: 536 us -> 555 us (1.035)
  waiting for transfers between devices: 385 us -> 393 us
  starting transfers between devices: 14.6 us -> 22 us
    all_to_all x0 -> x1, waiting for transfers between devices: none -> 70.8 us  [per_device(): lax.all_to_all(jnp.stack([tokens] * lax.axis_size('gy')), 'gy', 0, 0)]
    all_gather x1 -> x0, waiting for transfers between devices: 63.7 us -> none  [per_device(): whole_rows = lax.all_gather(tokens, 'gy', axis=2, tiled=True)]
    all_to_all x0 -> x1, starting transfers between devices: none -> 7.41 us  [per_device(): lax.all_to_all(jnp.stack([tokens] * lax.axis_size('gy')), 'gy', 0, 0)]
where the time goes in v1:
time: 555 us; the launch traced here: 553 us
  waiting for transfers between devices  393 us (71%)
  local copies, waits for them, and re-layouts  50.8 us (9%)
  matrix products  44.2 us (8%)
  other arithmetic  30.1 us (5%)
  starting transfers between devices  22 us (4%)
  between operations  13.4 us (2%)
    reduce_scatter x1, waiting for transfers between devices, per_device(): lax.psum_scatter(rounded.astype(jnp.float32).astype(jnp.bfloat16), 'gy',...  118 us
    reduce_scatter x1, waiting for transfers between devices, per_device(): lax.psum_scatter(jnp.dot(blocks, joined, preferred_element_type=jnp.float...  75.6 us
    all_gather x1, waiting for transfers between devices, per_device(): lax.all_gather(hidden, 'gx', axis=0, tiled=True)  72.2 us
    all_to_all x1, waiting for transfers between devices, per_device(): lax.all_to_all(jnp.stack([tokens] * lax.axis_size('gy')), 'gy', 0, 0)  70.8 us
    all_to_all x1, waiting for transfers between devices, per_device(): lax.all_to_all(feedforward_part.astype(jnp.bfloat16), 'gx', split_axis=0,...  24 us
    all_to_all x1, waiting for transfers between devices, per_device(): lax.all_to_all(normed, 'gx', split_axis=1, concat_axis=0, tiled=True)  23.7 us
    dot_general x1, matrix products, per_device(): jnp.dot(blocks, joined, preferred_element_type=jnp.float32)  22.6 us
    dot_general x1, matrix products, per_device(): jnp.dot(lax.all_gather(hidden, 'gx', axis=0, tiled=True), down_weight, pr...  15.5 us
  transfers between devices with their start and end apart: 8, of which 7 were waited for; matrix products, arithmetic and copies ran while one was open for 10% of the time, Pallas kernels for 0%

profile of v1, /device:TPU:0, one launch (start us, length us, event | category | flops | bytes accessed | tf_op | source)
XLA Modules:
  0.0 553.2 jit_solution(6784538111815050950)
XLA Ops:
  6.5 1.3 copy.28
  7.8 1.9 stack.8
  9.7 7.4 %all-to-all-start = ((bf16[8,1,256,768]{2,3,1,0:T(8,128)(2,1)}), bf16[8,1,256,768]{2,3,1,0:T(8,128)(2,1)}, u32[]{:S(2)}, u32[]{:S(2)}) async-start(bf16[8,1,256,768]{2,3,1,0:T(8,128)(2,1)} %stack.8), calls=%async_computation | async-start | bytes 6291456 | tf_op jit(solution)/shard_map/all_to_all | solution.py:36
  17.1 70.8 %all-to-all-done = bf16[8,1,256,768]{2,3,1,0:T(8,128)(2,1)} async-done(((bf16[8,1,256,768]{2,3,1,0:T(8,128)(2,1)}), bf16[8,1,256,768]{2,3,1,0:T(8,128)(2,1)}, u32[]{:S(2)}, u32[]{:S(2)}) %all-to-all-start) | async-done | bytes 3145760 | tf_op jit(solution)/shard_map/all_to_all | solution.py:36
  87.9 2.7 fusion.19
  90.7 2.4 bitcast_convert_fusion
  93.1 1.3 fusion.8
  94.4 2.1 multiply_convert_fusion
  96.5 4.7 all-to-all-start.1
  101.2 6.6 %copy.31 = bf16[1536,3,512]{0,2,1:T(8,128)(2,1)} copy(bf16[1536,3,512]{2,0,1:T(8,128)(2,1)} %param.12) | data formatting | bytes 9437184 | tf_op args[2]
  107.9 6.6 %copy.32 = bf16[1536,1536]{1,0:T(8,128)(2,1)} copy(bf16[1536,1536]{0,1:T(8,128)(2,1)} %bitcast.82) | data formatting | bytes 9437184 | tf_op jit(solution)/shard_map/reshape | solution.py:49
  114.5 23.7 %all-to-all-done.1 = bf16[256,4,1536]{0,2,1:T(8,128)(2,1)} async-done(((bf16[256,4,1536]{0,2,1:T(8,128)(2,1)}), bf16[256,4,1536]{0,2,1:T(8,128)(2,1)}, u32[]{:S(2)}, u32[]{:S(2)}) %all-to-all-start.1) | async-done | bytes 3145760 | tf_op jit(solution)/shard_map/all_to_all | solution.py:45
  138.2 4.7 copy.30
  142.8 22.6 %fusion.4 = bf16[1024,4608]{1,0:T(8,128)(2,1)} fusion(bf16[1024,1536]{1,0:T(8,128)(2,1)} %bitcast.85, bf16[1536,3072]{1,0:T(8,128)(2,1)} %param.13, bf16[1536,1536]{1,0:T(8,128)(2,1)} %copy.32), kind=kOutput, calls=%fused_computation.4 | convolution fusion | flops 14528544768 | bytes 26738688 | tf_op jit(solution)/shard_map/dot_general | solution.py:52
  166.1 75.6 %reduce-scatter.3.cloned.1.call-done = bf16[256,4608]{1,0:T(8,128)(2,1)} async-done(((bf16[1024,4608]{1,0:T(8,128)(2,1)}), bf16[256,4608]{1,0:T(8,128)(2,1)}) %reduce-scatter.3.cloned.1.call-update) | async-done | bytes 2359312 | tf_op jit(solution)/shard_map/reduce_scatter | solution.py:51
  241.7 1.2 fusion.38
  245.5 2.2 convert_element_type.100
  251.3 8.6 %fusion.11 = bf16[256,3072]{1,0:T(8,128)(2,1)} fusion(f32[256,4608]{1,0:T(8,128)} %copy-done.2), kind=kLoop, calls=%fused_computation.15 | loop fusion | flops 51118080 | bytes 4718592 | tf_op jit(solution)/shard_map/convert_element_type | solution.py:60
  259.9 8.3 %all-gather.3.cloned.1.call-done = bf16[1024,512]{0,1:T(8,128)(2,1)} async-done(((bf16[256,512]{0,1:T(8,128)(2,1)}), bf16[1024,512]{0,1:T(8,128)(2,1)}) %all-gather.3.cloned.1.call-update) | async-done | bytes 1048592 | tf_op jit(solution)/shard_map/all_gather | solution.py:74
  268.2 4.7 convolution_convert_fusion.1
  272.9 4.7 all-to-all-start.2
  277.6 72.2 %all-gather.5.cloned.1.call-done = bf16[1024,3072]{1,0:T(8,128)(2,1)} async-done(((bf16[256,3072]{1,0:T(8,128)(2,1)}), bf16[1024,3072]{1,0:T(8,128)(2,1)}) %all-gather.5.cloned.1.call-update) | async-done | bytes 6291472 | tf_op jit(solution)/shard_map/all_gather | solution.py:79
  349.9 15.5 %convolution_convert_fusion = bf16[1024,1536]{1,0:T(8,128)(2,1)} fusion(bf16[1024,3072]{1,0:T(8,128)(2,1)} %all-gather.5.cloned.1.call-done, bf16[3072,1536]{1,0:T(8,128)(2,1)} %param.17), kind=kOutput, calls=%fused_computation.11 | convolution fusion | flops 9665249280 | bytes 18874368 | tf_op jit(solution)/shard_map/dot_general | solution.py:78
  365.4 4.9 all-to-all-start.3
  370.3 6.0 %copy.37 = bf16[256,4,1536]{2,1,0:T(4,128)(2,1)} copy(bf16[256,4,1536]{2,0,1:T(8,128)(2,1)} %bitcast.15) | data formatting | bytes 6291456 | tf_op jit(solution)/shard_map/all_to_all | solution.py:84
  376.3 6.9 %stack.9 = bf16[1,256,6144]{2,1,0:T(8,128)(2,1)} reshape(bf16[256,4,1536]{2,1,0:T(4,128)(2,1)} %copy.37) | data formatting | bytes 6291456 | tf_op jit(solution)/shard_map/stack | solution.py:91
  383.3 24.0 %all-to-all-done.3 = bf16[4,256,1536]{2,1,0:T(8,128)(2,1)} async-done(((bf16[4,256,1536]{2,1,0:T(8,128)(2,1)}), bf16[4,256,1536]{2,1,0:T(8,128)(2,1)}, u32[]{:S(2)}, u32[]{:S(2)}) %all-to-all-start.3) | async-done | bytes 3145760 | tf_op jit(solution)/shard_map/all_to_all | solution.py:87
  407.3 6.0 %copy.38 = bf16[256,4,1536]{2,1,0:T(4,128)(2,1)} copy(bf16[256,4,1536]{2,0,1:T(8,128)(2,1)} %bitcast.17) | data formatting | bytes 6291456 | tf_op jit(solution)/shard_map/all_to_all | solution.py:87
  413.2 6.9 %stack.10 = bf16[1,256,6144]{2,1,0:T(8,128)(2,1)} reshape(bf16[256,4,1536]{2,1,0:T(4,128)(2,1)} %copy.38) | data formatting | bytes 6291456 | tf_op jit(solution)/shard_map/stack | solution.py:91
  420.2 6.1 %pad_maximum_fusion = bf16[2,256,6144]{2,1,0:T(8,128)(2,1)} fusion(bf16[1,256,6144]{2,1,0:T(8,128)(2,1)} %stack.10, bf16[1,256,6144]{2,1,0:T(8,128)(2,1)} %stack.9), kind=kLoop, calls=%fused_computation.5 | loop fusion | flops 3145728 | bytes 12582912 | tf_op jit(solution)/shard_map/stack | solution.py:91
  426.3 118.1 %reduce-scatter.5.cloned.1.call-done = bf16[2,256,768]{2,1,0:T(8,128)(2,1)} async-done(((bf16[2,256,6144]{2,1,0:T(8,128)(2,1)}), bf16[2,256,768]{2,1,0:T(8,128)(2,1)}) %reduce-scatter.5.cloned.1.call-update) | async-done | bytes 786448 | tf_op jit(solution)/shard_map/reduce_scatter | solution.py:93
  544.4 1.2 convert_element_type.110
  (52 shorter events, 7.9 us)
Async XLA Ops:
  6.5 261.7 %copy-start = (bf16[512,1536]{1,0:T(8,128)(2,1)S(1)}, bf16[512,1536]{1,0:T(8,128)(2,1)}, u32[]{:S(2)}) copy-start(bf16[512,1536]{1,0:T(8,128)(2,1)} %param.16) | copy-start | bytes 4718596
  9.7 7.4 %copy-start.6 = (f32[6144]{0:T(1024)S(1)}, f32[6144]{0:T(1024)}, u32[]{:S(2)}) copy-start(f32[6144]{0:T(1024)} %param.11) | copy-start | bytes 73732
  9.7 78.2 %all-to-all-start = ((bf16[8,1,256,768]{2,3,1,0:T(8,128)(2,1)}), bf16[8,1,256,768]{2,3,1,0:T(8,128)(2,1)}, u32[]{:S(2)}, u32[]{:S(2)}) async-start(bf16[8,1,256,768]{2,3,1,0:T(8,128)(2,1)} %stack.8), calls=%async_computation | async-start | bytes 6291456 | tf_op jit(solution)/shard_map/all_to_all | solution.py:36
  96.5 41.6 %all-to-all-start.1 = ((bf16[256,4,1536]{0,2,1:T(8,128)(2,1)}), bf16[256,4,1536]{0,2,1:T(8,128)(2,1)}, u32[]{:S(2)}, u32[]{:S(2)}) async-start(bf16[256,4,1536]{0,2,1:T(8,128)(2,1)} %multiply_convert_fusion), calls=%async_computation.1 | async-start | bytes 6291456 | tf_op jit(solution)/shard_map/all_to_all | solution.py:45
  101.2 140.5 %reduce-scatter.3.cloned.1.call-start = ((), (), s32[]{:S(2)}) async-start(), calls=%async_computation.6 | async-start | bytes 11796480 | tf_op jit(solution)/shard_map/reduce_scatter | solution.py:51
  165.5 0.7 copy-start.7
  165.5 0.7 copy-start.8
  165.5 102.7 %all-gather.3.cloned.1.call-start = ((), (), s32[]{:S(2)}) async-start(), calls=%async_computation.7 | async-start | bytes 1310720 | tf_op jit(solution)/shard_map/all_gather | solution.py:74
  242.9 2.5 slice-start
  247.7 2.1 copy-start.2
  251.2 98.7 %all-gather.5.cloned.1.call-start = ((), (), s32[]{:S(2)}) async-start(), calls=%async_computation.8 | async-start | bytes 7864320 | tf_op jit(solution)/shard_map/all_gather | solution.py:79
  272.9 92.5 %all-to-all-start.2 = ((bf16[4,256,1536]{2,1,0:T(8,128)(2,1)}), bf16[4,256,1536]{2,1,0:T(8,128)(2,1)}, u32[]{:S(2)}, u32[]{:S(2)}) async-start(bf16[4,256,1536]{2,1,0:T(8,128)(2,1)} %bitcast.84), calls=%async_computation.3 | async-start | bytes 6291456 | tf_op jit(solution)/shard_map/all_to_all | solution.py:84
  365.4 41.8 %all-to-all-start.3 = ((bf16[4,256,1536]{2,1,0:T(8,128)(2,1)}), bf16[4,256,1536]{2,1,0:T(8,128)(2,1)}, u32[]{:S(2)}, u32[]{:S(2)}) async-start(bf16[4,256,1536]{2,1,0:T(8,128)(2,1)} %bitcast.83), calls=%async_computation.4 | async-start | bytes 6291456 | tf_op jit(solution)/shard_map/all_to_all | solution.py:87
  370.3 174.1 %reduce-scatter.5.cloned.1.call-start = ((), (), s32[]{:S(2)}) async-start(), calls=%async_computation.9 | async-start | bytes 7077888 | tf_op jit(solution)/shard_map/reduce_scatter | solution.py:93
  426.2 119.4 %copy-start.3 = (bf16[1,256,768]{2,1,0:T(8,128)(2,1)S(1)}, bf16[1,256,768]{2,1,0:T(8,128)(2,1)}, u32[]{:S(2)}) copy-start(bf16[1,256,768]{2,1,0:T(8,128)(2,1)} %param.10) | copy-start | bytes 1179652
  426.2 119.4 %copy-start.4 = (s32[1,256,768]{2,1,0:T(8,128)S(1)}, s32[1,256,768]{2,1,0:T(8,128)}, u32[]{:S(2)}) copy-start(s32[1,256,768]{2,1,0:T(8,128)} %param.19) | copy-start | bytes 2359300
  426.2 119.4 %copy-start.5 = (s32[1,256,768]{2,1,0:T(8,128)S(1)}, s32[1,256,768]{2,1,0:T(8,128)}, u32[]{:S(2)}) copy-start(s32[1,256,768]{2,1,0:T(8,128)} %param.18) | copy-start | bytes 2359300
  426.3 120.4 %copy-start.1 = (bf16[512,1536]{1,0:T(8,128)(2,1)S(1)}, bf16[512,1536]{1,0:T(8,128)(2,1)}, u32[]{:S(2)}) copy-start(bf16[512,1536]{1,0:T(8,128)(2,1)} %param.16) | copy-start | bytes 4718596
Sparse Core Ops, SparseCore 0:
  165.6 76.0 reduce-scatter.2
  251.3 16.8 all-gather.2
  269.8 80.0 all-gather.4
  426.4 117.9 reduce-scatter.4
